TPU v7x, 32 devices: a whole 2x2x4 slice. The times are simulated.
32 devices in a mesh: rep: 8 (over y, x, core), shard: 4 (over z).
Axes of the slice: x: 2, y: 2, z: 4, core: 2. Of those that a mesh axis runs over, the one named last changes fastest.
Arguments:
- tokens: bfloat16 [16384, 1536], P(('rep', 'shard')), may hold values from -6 to 6
- cotangent: bfloat16 [16384, 1536], P(('rep', 'shard')), may hold values from -6 to 6
- norm_first: bfloat16 [1536], P('shard'), may hold values from 0.5 to 1.5
- branch_weight: bfloat16 [1536, 2048], P(None, 'shard'), may hold values from -0.15625 to 0.15625
- gelu_weight: bfloat16 [1536, 2048], P(None, 'shard'), may hold values from -0.15625 to 0.15625
- conv_weight: bfloat16 [4, 2048], P(None, 'shard'), may hold values from -2.5 to 2.5
- conv_bias: bfloat16 [2048], P('shard'), may hold values from -2.5 to 2.5
- gate_weight: bfloat16 [16, 128, 256], P('shard'), may hold values from -0.5 to 0.5
- gate_bias: bfloat16 [16, 256], P('shard'), may hold values from -2.5 to 2.5
- decay_param: bfloat16 [2048], P('shard'), may hold values from 2.1875 to 6.875
- merge_weight: bfloat16 [2048, 1536], P('shard'), may hold values from -0.375 to 0.375
- norm_second: bfloat16 [1536], P('shard'), may hold values from 0.5 to 1.5
- feed_gate: bfloat16 [1536, 4608], P(None, 'shard'), may hold values from -0.15625 to 0.15625
- feed_up: bfloat16 [1536, 4608], P(None, 'shard'), may hold values from -0.15625 to 0.15625
- feed_down: bfloat16 [4608, 1536], P('shard'), may hold values from -0.1875 to 0.1875
- down_branch: bfloat16 [1536, 128], P(None, 'shard'), may hold values from -0.15625 to 0.15625
- up_branch: bfloat16 [128, 2048], P('shard'), may hold values from -0.75 to 0.75
- down_gelu: bfloat16 [1536, 128], P(None, 'shard'), may hold values from -0.15625 to 0.15625
- up_gelu: bfloat16 [128, 2048], P('shard'), may hold values from -0.75 to 0.75
- down_gates: bfloat16 [2048, 128], P(None, 'shard'), may hold values from -0.125 to 0.125
- up_gates: bfloat16 [128, 4096], P('shard'), may hold values from -0.75 to 0.75
- down_merge: bfloat16 [2048, 128], P(None, 'shard'), may hold values from -0.125 to 0.125
- up_merge: bfloat16 [128, 1536], P('shard'), may hold values from -0.75 to 0.75
- down_feed_gate: bfloat16 [1536, 128], P(None, 'shard'), may hold values from -0.15625 to 0.15625
- up_feed_gate: bfloat16 [128, 4608], P('shard'), may hold values from -0.75 to 0.75
- down_feed_up: bfloat16 [1536, 128], P(None, 'shard'), may hold values from -0.15625 to 0.15625
- up_feed_up: bfloat16 [128, 4608], P('shard'), may hold values from -0.75 to 0.75
- down_feed_down: bfloat16 [4608, 128], P(None, 'shard'), may hold values from -0.09375 to 0.09375
- up_feed_down: bfloat16 [128, 1536], P('shard'), may hold values from -0.75 to 0.75
- seq_lengths: int32 [32, 4], P(('rep', 'shard')), may hold values from 1 to 256, 384 in all within a row
- adapter_index: int32 [32, 4], P(('rep', 'shard')), may hold values from 0 to 7
- deal_order: int32 [8, 2048], P('rep'), may hold values from 0 to 2047, as said below
Outputs:
- layer_out: float32 [16384, 1536], P(('rep', 'shard'))
- grad_tokens: float32 [16384, 1536], P(('rep', 'shard'))
- grad_down_branch: float32 [1536, 128], P(None, 'shard')
- grad_up_branch: float32 [128, 2048], P('shard')
- grad_down_gelu: float32 [1536, 128], P(None, 'shard')
- grad_up_gelu: float32 [128, 2048], P('shard')
- grad_down_gates: float32 [2048, 128], P(None, 'shard')
- grad_up_gates: float32 [128, 4096], P('shard')
- grad_down_merge: float32 [2048, 128], P(None, 'shard')
- grad_up_merge: float32 [128, 1536], P('shard')
- grad_down_feed_gate: float32 [1536, 128], P(None, 'shard')
- grad_up_feed_gate: float32 [128, 4608], P('shard')
- grad_down_feed_up: float32 [1536, 128], P(None, 'shard')
- grad_up_feed_up: float32 [128, 4608], P('shard')
- grad_down_feed_down: float32 [4608, 128], P(None, 'shard')
- grad_up_feed_down: float32 [128, 1536], P('shard')
Inputs may be any that keep to these rules, and one draw needn't show every extreme that they name: Each row of deal_order is a permutation of 0 to 2047. Exactly 128 of the arrival rows of one device (rows b * 512 to b * 512 + 511 of its group) fill slots of each block of its group. `seq_lengths`: in every block the lengths sum to 384 and the longest is 256.
All inputs are finite; a program needn't handle non-finite values.
Results may differ from a plain program's by a relative error of at most 0.015.
Values may be sent and summed in bfloat16 or wider, within the bound.
A program may use at most 320 MiB of HBM per device.

v0:
```python
import jax
import jax.numpy as jnp
from jax import lax
from jax.sharding import PartitionSpec as P

H = 16
DH = 128
NA = 8
R = 16
NORM_EPSILON = 1e-06
DECAY_SCALE = 8.0


def matmul(left, right):
    return jnp.dot(left, right, preferred_element_type=jnp.float32)


def matmul_right_t(left, right):
    return lax.dot_general(
        left, right, (((1,), (1,)), ((), ())), preferred_element_type=jnp.float32
    )


def matmul_left_t(left, right):
    return lax.dot_general(
        left, right, (((0,), (0,)), ((), ())), preferred_element_type=jnp.float32
    )


def root_norm(values, gain):
    return (
        values * lax.rsqrt(jnp.mean(values * values, axis=-1, keepdims=True) + NORM_EPSILON) * gain
    )


def layout(lengths_row, index_row, slots_count):
    seq_count = lengths_row.shape[0]
    ends = jnp.cumsum(lengths_row)
    starts = ends - lengths_row
    slots = jnp.arange(slots_count, dtype=jnp.int32)
    segment = jnp.sum((slots[:, None] >= ends[None, :]).astype(jnp.int32), axis=1)
    start_all = jnp.concatenate([starts, ends[-1:]])
    member = segment[:, None] == jnp.arange(seq_count + 1, dtype=jnp.int32)[None, :]
    position = slots - jnp.sum(jnp.where(member, start_all[None, :], 0), axis=1)
    live_rows = segment < seq_count
    chosen = jnp.sum(jnp.where(member[:, :seq_count], index_row[None, :], 0), axis=1)
    adapter_hit = (chosen[:, None] == jnp.arange(NA, dtype=jnp.int32)[None, :]) & live_rows[:, None]
    adapter_mask = jnp.repeat(adapter_hit.astype(jnp.float32), R, axis=1)
    return (position, live_rows.astype(jnp.float32), adapter_mask)


def conv_apply(values, weight, bias, position):
    total = bias[None, :] + weight[0][None, :] * values
    for offset in range(1, weight.shape[0]):
        moved = jnp.concatenate(
            [jnp.zeros((offset, values.shape[1]), values.dtype), values[:-offset]], axis=0
        )
        keeper = (position >= offset).astype(values.dtype)[:, None]
        total = total + weight[offset][None, :] * moved * keeper
    return total


def combine(earlier, later):
    return (earlier[0] * later[0], later[0] * earlier[1] + later[1])


def recurrence(gate_logits, conv_out, gelu_in, decay, position):
    rows_count = conv_out.shape[0]
    shaped = gate_logits.reshape(rows_count, H, 2 * DH)
    input_gate = jax.nn.sigmoid(shaped[:, :, :DH]).reshape(rows_count, H * DH)
    rec_gate = jax.nn.sigmoid(shaped[:, :, DH:]).reshape(rows_count, H * DH)
    log_decay = -DECAY_SCALE * rec_gate * jax.nn.softplus(-decay)[None, :]
    decay_now = jnp.exp(log_decay)
    first = (position == 0)[:, None]
    scale_in = jnp.where(first, 1.0, jnp.sqrt(-jnp.expm1(2.0 * log_decay)))
    carried = jnp.where(first, 0.0, decay_now)
    driven = scale_in * input_gate * conv_out
    unused, state = lax.associative_scan(combine, (carried, driven), axis=0)
    return state * jax.nn.gelu(gelu_in)


def feed_mix(hidden_gate, hidden_up):
    return jax.nn.gelu(hidden_gate) * hidden_up


def local(
    tokens,
    cotangent,
    norm_first,
    branch_weight,
    gelu_weight,
    conv_weight,
    conv_bias,
    gate_weight,
    gate_bias,
    decay_param,
    merge_weight,
    norm_second,
    feed_gate,
    feed_up,
    feed_down,
    down_branch,
    up_branch,
    down_gelu,
    up_gelu,
    down_gates,
    up_gates,
    down_merge,
    up_merge,
    down_feed_gate,
    up_feed_gate,
    down_feed_up,
    up_feed_up,
    down_feed_down,
    up_feed_down,
    seq_lengths,
    adapter_index,
    deal_order,
):
    rows_here = tokens.shape[0]
    shards = lax.axis_size("shard")
    my_index = lax.axis_index("shard")
    deal_row = deal_order[0]
    group_rows = deal_row.shape[0]
    gathered = (
        lax.all_gather(tokens, "shard", axis=0, tiled=True),
        lax.all_gather(cotangent, "shard", axis=0, tiled=True),
    )
    my_picks = lax.dynamic_slice_in_dim(deal_row, my_index * rows_here, rows_here)
    work_in = jnp.take(gathered[0], my_picks, axis=0)
    work_cot = jnp.take(gathered[1], my_picks, axis=0)
    block_parts = (
        lax.all_gather(norm_first, "shard", axis=0, tiled=True),
        lax.all_gather(branch_weight, "shard", axis=1, tiled=True),
        lax.all_gather(gelu_weight, "shard", axis=1, tiled=True),
        lax.all_gather(conv_weight, "shard", axis=1, tiled=True),
        lax.all_gather(conv_bias, "shard", axis=0, tiled=True),
        lax.all_gather(gate_weight, "shard", axis=0, tiled=True),
        lax.all_gather(gate_bias, "shard", axis=0, tiled=True),
        lax.all_gather(decay_param, "shard", axis=0, tiled=True),
        lax.all_gather(merge_weight, "shard", axis=0, tiled=True),
    )
    (
        gain_first,
        weight_branch,
        weight_gelu,
        taps_conv,
        bias_conv,
        weight_gates,
        bias_gates,
        decay_all,
        weight_merge,
    ) = block_parts
    adapter_parts = (
        lax.all_gather(down_branch, "shard", axis=1, tiled=True),
        lax.all_gather(up_branch, "shard", axis=0, tiled=True),
        lax.all_gather(down_gelu, "shard", axis=1, tiled=True),
        lax.all_gather(up_gelu, "shard", axis=0, tiled=True),
        lax.all_gather(down_gates, "shard", axis=1, tiled=True),
        lax.all_gather(up_gates, "shard", axis=0, tiled=True),
        lax.all_gather(down_merge, "shard", axis=1, tiled=True),
        lax.all_gather(up_merge, "shard", axis=0, tiled=True),
        lax.all_gather(down_feed_gate, "shard", axis=1, tiled=True),
        lax.all_gather(up_feed_gate, "shard", axis=0, tiled=True),
        lax.all_gather(down_feed_up, "shard", axis=1, tiled=True),
        lax.all_gather(up_feed_up, "shard", axis=0, tiled=True),
        lax.all_gather(down_feed_down, "shard", axis=1, tiled=True),
        lax.all_gather(up_feed_down, "shard", axis=0, tiled=True),
    )
    (
        fact_down_branch,
        fact_up_branch,
        fact_down_gelu,
        fact_up_gelu,
        fact_down_gates,
        fact_up_gates,
        fact_down_merge,
        fact_up_merge,
        fact_down_fgate,
        fact_up_fgate,
        fact_down_fup,
        fact_up_fup,
        fact_down_fdown,
        fact_up_fdown,
    ) = adapter_parts
    position, live_rows, adapter_mask = layout(seq_lengths[0], adapter_index[0], rows_here)

    def adapter_forward(act, down, up):
        rank_part = (matmul(act, down) * adapter_mask).astype(jnp.bfloat16)
        return (rank_part, matmul(rank_part, up))

    def adapter_backward(grad_low, act, rank_part, up):
        grad_rank = (matmul_right_t(grad_low, up) * adapter_mask).astype(jnp.bfloat16)
        return (grad_rank, matmul_left_t(act, grad_rank), matmul_left_t(rank_part, grad_low))

    gain_first_f = gain_first.astype(jnp.float32)
    rows_in = work_in.astype(jnp.float32)
    normed_first, first_pull = jax.vjp(lambda values: root_norm(values, gain_first_f), rows_in)
    act_first = normed_first.astype(jnp.bfloat16)
    rank_branch, extra_branch = adapter_forward(act_first, fact_down_branch, fact_up_branch)
    branch = matmul(act_first, weight_branch) + extra_branch
    rank_gelu, extra_gelu = adapter_forward(act_first, fact_down_gelu, fact_up_gelu)
    gelu_in = matmul(act_first, weight_gelu) + extra_gelu
    taps_f = taps_conv.astype(jnp.float32)
    bias_f = bias_conv.astype(jnp.float32)
    conv_out, conv_pull = jax.vjp(
        lambda values: conv_apply(values, taps_f, bias_f, position), branch
    )
    conv_low = conv_out.astype(jnp.bfloat16)
    heads = conv_low.reshape(rows_here, H, DH)
    blockwise = jnp.einsum(
        "thd,hde->the", heads, weight_gates, preferred_element_type=jnp.float32
    ).reshape(rows_here, 2 * H * DH)
    rank_gates, extra_gates = adapter_forward(conv_low, fact_down_gates, fact_up_gates)
    gate_logits = blockwise + bias_gates.astype(jnp.float32).reshape(-1)[None, :] + extra_gates
    decay_f = decay_all.astype(jnp.float32)
    mixed, mixed_pull = jax.vjp(
        lambda logits, conv_in, gelu_part: recurrence(
            logits, conv_in, gelu_part, decay_f, position
        ),
        gate_logits,
        conv_out,
        gelu_in,
    )
    mixed_low = mixed.astype(jnp.bfloat16)
    rank_merge, extra_merge = adapter_forward(mixed_low, fact_down_merge, fact_up_merge)
    resid = rows_in + matmul(mixed_low, weight_merge) + extra_merge
    feed_parts = (
        lax.all_gather(norm_second, "shard", axis=0, tiled=True),
        lax.all_gather(feed_gate, "shard", axis=1, tiled=True),
        lax.all_gather(feed_up, "shard", axis=1, tiled=True),
        lax.all_gather(feed_down, "shard", axis=0, tiled=True),
    )
    gain_second, weight_fgate, weight_fup, weight_fdown = feed_parts
    gain_second_f = gain_second.astype(jnp.float32)
    normed_second, second_pull = jax.vjp(lambda values: root_norm(values, gain_second_f), resid)
    act_second = normed_second.astype(jnp.bfloat16)
    rank_fgate, extra_fgate = adapter_forward(act_second, fact_down_fgate, fact_up_fgate)
    hidden_gate = matmul(act_second, weight_fgate) + extra_fgate
    rank_fup, extra_fup = adapter_forward(act_second, fact_down_fup, fact_up_fup)
    hidden_up = matmul(act_second, weight_fup) + extra_fup
    hidden, hidden_pull = jax.vjp(feed_mix, hidden_gate, hidden_up)
    hidden_low = hidden.astype(jnp.bfloat16)
    rank_fdown, extra_fdown = adapter_forward(hidden_low, fact_down_fdown, fact_up_fdown)
    work_out = (resid + matmul(hidden_low, weight_fdown) + extra_fdown) * live_rows[:, None]
    grad_out = work_cot.astype(jnp.float32) * live_rows[:, None]
    grad_out_low = grad_out.astype(jnp.bfloat16)
    grad_rank_fdown, grad_down_fdown, grad_up_fdown = adapter_backward(
        grad_out_low, hidden_low, rank_fdown, fact_up_fdown
    )
    grad_hidden = matmul_right_t(grad_out_low, weight_fdown) + matmul_right_t(
        grad_rank_fdown, fact_down_fdown
    )
    grad_hgate, grad_hup = hidden_pull(grad_hidden)
    grad_hgate_low = grad_hgate.astype(jnp.bfloat16)
    grad_hup_low = grad_hup.astype(jnp.bfloat16)
    grad_rank_fgate, grad_down_fgate, grad_up_fgate = adapter_backward(
        grad_hgate_low, act_second, rank_fgate, fact_up_fgate
    )
    grad_rank_fup, grad_down_fup, grad_up_fup = adapter_backward(
        grad_hup_low, act_second, rank_fup, fact_up_fup
    )
    grad_second = (
        matmul_right_t(grad_hgate_low, weight_fgate)
        + matmul_right_t(grad_hup_low, weight_fup)
        + matmul_right_t(grad_rank_fgate, fact_down_fgate)
        + matmul_right_t(grad_rank_fup, fact_down_fup)
    )
    grad_resid = grad_out + second_pull(grad_second)[0]
    grad_resid_low = grad_resid.astype(jnp.bfloat16)
    grad_rank_merge, grad_down_merge, grad_up_merge = adapter_backward(
        grad_resid_low, mixed_low, rank_merge, fact_up_merge
    )
    grad_mixed = matmul_right_t(grad_resid_low, weight_merge) + matmul_right_t(
        grad_rank_merge, fact_down_merge
    )
    grad_logits, grad_conv_direct, grad_gelu_in = mixed_pull(grad_mixed)
    grad_logits_low = grad_logits.astype(jnp.bfloat16)
    grad_rank_gates, grad_down_gates, grad_up_gates = adapter_backward(
        grad_logits_low, conv_low, rank_gates, fact_up_gates
    )
    grad_heads = jnp.einsum(
        "the,hde->thd",
        grad_logits_low.reshape(rows_here, H, 2 * DH),
        weight_gates,
        preferred_element_type=jnp.float32,
    ).reshape(rows_here, H * DH)
    grad_conv = grad_conv_direct + grad_heads + matmul_right_t(grad_rank_gates, fact_down_gates)
    grad_branch = conv_pull(grad_conv)[0]
    grad_branch_low = grad_branch.astype(jnp.bfloat16)
    grad_gelu_low = grad_gelu_in.astype(jnp.bfloat16)
    grad_rank_branch, grad_down_branch, grad_up_branch = adapter_backward(
        grad_branch_low, act_first, rank_branch, fact_up_branch
    )
    grad_rank_gelu, grad_down_gelu, grad_up_gelu = adapter_backward(
        grad_gelu_low, act_first, rank_gelu, fact_up_gelu
    )
    grad_first = (
        matmul_right_t(grad_branch_low, weight_branch)
        + matmul_right_t(grad_gelu_low, weight_gelu)
        + matmul_right_t(grad_rank_branch, fact_down_branch)
        + matmul_right_t(grad_rank_gelu, fact_down_gelu)
    )
    grad_work = grad_resid + first_pull(grad_first)[0]
    collected = (
        lax.all_gather(work_out, "shard", axis=0, tiled=True),
        lax.all_gather(grad_work, "shard", axis=0, tiled=True),
    )
    inverse = (
        jnp.zeros((group_rows,), jnp.int32)
        .at[deal_row]
        .set(jnp.arange(group_rows, dtype=jnp.int32))
    )
    my_rows = lax.dynamic_slice_in_dim(inverse, my_index * rows_here, rows_here)
    layer_out = jnp.take(collected[0], my_rows, axis=0)
    grad_tokens = jnp.take(collected[1], my_rows, axis=0)
    part_width = grad_down_branch.shape[1] // shards
    summed = lax.psum(
        (
            grad_down_branch,
            grad_up_branch,
            grad_down_gelu,
            grad_up_gelu,
            grad_down_gates,
            grad_up_gates,
            grad_down_merge,
            grad_up_merge,
            grad_down_fgate,
            grad_up_fgate,
            grad_down_fup,
            grad_up_fup,
            grad_down_fdown,
            grad_up_fdown,
        ),
        ("rep", "shard"),
    )
    owned = tuple(
        (
            lax.dynamic_slice_in_dim(
                summed[number], my_index * part_width, part_width, 1 - number % 2
            )
            for number in range(14)
        )
    )
    return (
        layer_out,
        grad_tokens,
        owned[0],
        owned[1],
        owned[2],
        owned[3],
        owned[4],
        owned[5],
        owned[6],
        owned[7],
        owned[8],
        owned[9],
        owned[10],
        owned[11],
        owned[12],
        owned[13],
    )


def solution(mesh):
    in_specs = (
        P(("rep", "shard"), None),
        P(("rep", "shard"), None),
        P("shard"),
        P(None, "shard"),
        P(None, "shard"),
        P(None, "shard"),
        P("shard"),
        P("shard", None, None),
        P("shard", None),
        P("shard"),
        P("shard", None),
        P("shard"),
        P(None, "shard"),
        P(None, "shard"),
        P("shard", None),
        P(None, "shard"),
        P("shard", None),
        P(None, "shard"),
        P("shard", None),
        P(None, "shard"),
        P("shard", None),
        P(None, "shard"),
        P("shard", None),
        P(None, "shard"),
        P("shard", None),
        P(None, "shard"),
        P("shard", None),
        P(None, "shard"),
        P("shard", None),
        P(("rep", "shard"), None),
        P(("rep", "shard"), None),
        P("rep", None),
    )
    out_specs = (
        P(("rep", "shard"), None),
        P(("rep", "shard"), None),
        P(None, "shard"),
        P("shard", None),
        P(None, "shard"),
        P("shard", None),
        P(None, "shard"),
        P("shard", None),
        P(None, "shard"),
        P("shard", None),
        P(None, "shard"),
        P("shard", None),
        P(None, "shard"),
        P("shard", None),
        P(None, "shard"),
        P("shard", None),
    )
    return jax.shard_map(local, mesh=mesh, in_specs=in_specs, out_specs=out_specs, check_vma=False)
```

profile of v0, /device:TPU:0, one launch (start us, length us, event | category | flops | bytes accessed | tf_op | source)
XLA Modules:
  0.0 3010.1 jit_solution(17063541124897532782)
XLA Ops:
  19.0 15.6 all-gather.1
  35.0 17.7 all_gather.98
  52.7 23.4 all_gather.99
  76.9 16.7 all_gather.95
  93.6 14.6 all-gather
  108.3 20.1 all_gather.102
  128.4 15.4 all-gather.2
  143.8 12.0 all-gather.3
  156.5 17.4 all_gather.106
  173.8 23.5 all_gather.107
  197.3 24.9 all_gather.109
  222.2 22.7 all_gather.110
  244.9 12.1 all-gather.4
  257.6 20.9 all_gather.116
  278.5 22.2 all_gather.113
  300.7 15.2 all_gather.120
  347.6 8.9 copy.113
  362.9 8.3 add_add_fusion
  371.1 9.3 copy.142
  398.1 11.7 exponential_select_fusion
  409.8 9.8 slice.325
  419.6 9.8 slice.326
  429.5 9.8 slice.324
  439.3 9.8 slice.328
  556.3 10.1 slice.323
  566.5 10.1 slice.388
  598.7 8.7 pad.364
  616.3 16.5 pad.367
  638.7 16.5 pad.366
  678.3 31.0 %all-gather.47.cloned.1.call-done = bf16[2048,1536]{1,0:T(8,128)(2,1)} async-done(((bf16[512,1536]{1,0:T(8,128)(2,1)}), bf16[2048,1536]{1,0:T(8,128)(2,1)}) %all-gather.47.cloned.1.call-update) | async-done | bytes 6291472 | tf_op jit(solution)/shard_map/all_gather | solution.py:127
  709.3 8.2 gather_fusion.2
  720.0 233.1 %all-gather.37.cloned.1.call-done = bf16[1536,4608]{1,0:T(8,128)(2,1)} async-done(((bf16[1536,1152]{1,0:T(8,128)(2,1)}), bf16[1536,4608]{1,0:T(8,128)(2,1)}) %all-gather.37.cloned.1.call-update) | async-done | bytes 14155792 | tf_op jit(solution)/shard_map/all_gather | solution.py:231
  953.1 12.9 fusion.130
  965.9 230.9 %all-gather.33.cloned.1.call-done = bf16[1536,4608]{1,0:T(8,128)(2,1)} async-done(((bf16[1536,1152]{1,0:T(8,128)(2,1)}), bf16[1536,4608]{1,0:T(8,128)(2,1)}) %all-gather.33.cloned.1.call-update) | async-done | bytes 14155792 | tf_op jit(solution)/shard_map/all_gather | solution.py:230
  1196.8 12.8 fusion.129
  1209.7 17.2 all-gather.39.cloned.1.call-done
  1226.9 9.0 convolution_add_fusion.1
  1235.9 22.2 all-gather.35.cloned.1.call-done
  1258.1 10.0 convolution_add_fusion.2
  1268.1 234.5 %all-gather.41.cloned.1.call-done = bf16[4608,1536]{1,0:T(8,128)(2,1)} async-done(((bf16[1152,1536]{1,0:T(8,128)(2,1)}), bf16[4608,1536]{1,0:T(8,128)(2,1)}) %all-gather.41.cloned.1.call-update) | async-done | bytes 14155792 | tf_op jit(solution)/shard_map/all_gather | solution.py:232
  1502.6 13.4 fusion.95
  1516.0 16.8 all-gather.43.cloned.1.call-done
  1532.8 17.3 multiply_convert_fusion
  1550.1 13.4 fusion.131
  1564.9 10.3 convolution_add_fusion.12
  1598.4 9.8 slice.389
  1615.1 9.8 slice.390
  1714.0 8.8 pad.425
  1727.5 8.6 pad.450
  1736.2 8.7 pad.375
  1749.8 11.2 multiply_add_fusion.1
  1763.9 16.6 pad.426
  1780.5 16.5 pad.427
  1797.0 16.6 pad.451
  1813.6 16.6 pad.452
  1830.2 16.9 pad.370
  1847.1 16.9 pad.428
  1864.0 18.5 multiply_multiply_fusion.5
  1977.3 12.4 convolution_add_fusion.13
  2019.8 528.0 %all-reduce.96.cloned.1.call-done = (f32[1536,128]{0,1:T(8,128)}, f32[128,2048]{1,0:T(8,128)}, f32[1536,128]{0,1:T(8,128)}, f32[128,2048]{1,0:T(8,128)}, f32[204...) async-done(((f32[1536,128]{0,1:T(8,128)}, ...) | async-done | bytes 18087952 | tf_op jit(solution)/shard_map/psum | solution.py:318
  2563.3 207.1 %all-gather.45.cloned.1.call-done = f32[2048,1536]{1,0:T(8,128)} async-done(((f32[512,1536]{1,0:T(8,128)}), f32[2048,1536]{1,0:T(8,128)}) %all-gather.45.cloned.1.call-update) | async-done | bytes 12582928 | tf_op jit(solution)/shard_map/all_gather | solution.py:306
  2770.3 8.3 gather_fusion.1
  2778.6 210.2 %all-gather.49.cloned.1.call-done = f32[2048,1536]{1,0:T(8,128)} async-done(((f32[512,1536]{1,0:T(8,128)}), f32[2048,1536]{1,0:T(8,128)}) %all-gather.49.cloned.1.call-update) | async-done | bytes 12582928 | tf_op jit(solution)/shard_map/all_gather | solution.py:307
  2988.8 9.1 gather_fusion.3
  (797 shorter events, 515.4 us)
Async XLA Ops:
  7.2 310.7 %all-gather.21.cloned.1.call-start = ((), (), s32[]{:S(2)}) async-start(), calls=%async_computation | async-start | bytes 7864320 | tf_op jit(solution)/shard_map/all_gather | solution.py:126
  7.9 321.1 %all-gather.23.cloned.1.call-start = ((), (), s32[]{:S(2)}) async-start(), calls=%async_computation.1 | async-start | bytes 7864320 | tf_op jit(solution)/shard_map/all_gather | solution.py:134
  8.7 332.4 %all-gather.25.cloned.1.call-start = ((), (), s32[]{:S(2)}) async-start(), calls=%async_computation.2 | async-start | bytes 1310720 | tf_op jit(solution)/shard_map/all_gather | solution.py:138
  9.4 353.5 %all-gather.27.cloned.1.call-start = ((), (), s32[]{:S(2)}) async-start(), calls=%async_computation.3 | async-start | bytes 1310720 | tf_op jit(solution)/shard_map/all_gather | solution.py:160
  10.0 645.9 %all-gather.29.cloned.1.call-start = ((), (), s32[]{:S(2)}) async-start(), calls=%async_computation.4 | async-start | bytes 7864320 | tf_op jit(solution)/shard_map/all_gather | solution.py:135
  10.6 657.5 %all-gather.31.cloned.1.call-start = ((), (), s32[]{:S(2)}) async-start(), calls=%async_computation.5 | async-start | bytes 7864320 | tf_op jit(solution)/shard_map/all_gather | solution.py:141
  11.1 698.2 %all-gather.47.cloned.1.call-start = ((), (), s32[]{:S(2)}) async-start(), calls=%async_computation.13 | async-start | bytes 7864320 | tf_op jit(solution)/shard_map/all_gather | solution.py:127
  11.9 941.2 %all-gather.37.cloned.1.call-start = ((), (), s32[]{:S(2)}) async-start(), calls=%async_computation.8 | async-start | bytes 17694720 | tf_op jit(solution)/shard_map/all_gather | solution.py:231
  12.7 22.1 copy-start.211
  12.7 22.3 copy-start.168
  12.7 40.0 %copy-start.157 = (bf16[32,2048]{1,0:T(8,128)(2,1)S(1)}, bf16[32,2048]{1,0:T(8,128)(2,1)}, u32[]{:S(2)}) copy-start(bf16[32,2048]{1,0:T(8,128)(2,1)} %param.52) | copy-start | bytes 393220
  12.7 64.2 %copy-start.204 = (bf16[4,512]{1,0:T(4,128)(2,1)S(1)}, bf16[4,512]{1,0:T(4,128)(2,1)}, u32[]{:S(2)}) copy-start(bf16[4,512]{1,0:T(4,128)(2,1)} %param.41) | copy-start | bytes 12292
  12.7 80.9 %copy-start.206 = (bf16[512]{0:T(512)(128)(2,1)S(1)}, bf16[512]{0:T(512)(128)(2,1)}, u32[]{:S(2)}) copy-start(bf16[512]{0:T(512)(128)(2,1)} %param.42) | copy-start | bytes 3076
  12.7 1184.1 %all-gather.33.cloned.1.call-start = ((), (), s32[]{:S(2)}) async-start(), calls=%async_computation.6 | async-start | bytes 17694720 | tf_op jit(solution)/shard_map/all_gather | solution.py:230
  13.4 94.8 %copy-start.158 = (bf16[2048,32]{0,1:T(8,128)(2,1)S(1)}, bf16[2048,32]{0,1:T(8,128)(2,1)}, u32[]{:S(2)}) copy-start(bf16[2048,32]{0,1:T(8,128)(2,1)} %param.55) | copy-start | bytes 393220
  13.5 114.9 %copy-start.205 = (bf16[4,256]{1,0:T(4,128)(2,1)S(1)}, bf16[4,256]{1,0:T(4,128)(2,1)}, u32[]{:S(2)}) copy-start(bf16[4,256]{1,0:T(4,128)(2,1)} %param.44) | copy-start | bytes 6148
  13.5 130.4 %copy-start.207 = (bf16[512]{0:T(512)(128)(2,1)S(1)}, bf16[512]{0:T(512)(128)(2,1)}, u32[]{:S(2)}) copy-start(bf16[512]{0:T(512)(128)(2,1)} %param.45) | copy-start | bytes 3076
  13.5 143.0 %copy-start.169 = (bf16[1536,32]{0,1:T(8,128)(2,1)S(1)}, bf16[1536,32]{0,1:T(8,128)(2,1)}, u32[]{:S(2)}) copy-start(bf16[1536,32]{0,1:T(8,128)(2,1)} %param.53) | copy-start | bytes 294916
  13.5 160.3 %copy-start.159 = (bf16[32,2048]{1,0:T(8,128)(2,1)S(1)}, bf16[32,2048]{1,0:T(8,128)(2,1)}, u32[]{:S(2)}) copy-start(bf16[32,2048]{1,0:T(8,128)(2,1)} %param.54) | copy-start | bytes 393220
  13.5 1213.4 %all-gather.39.cloned.1.call-start = ((), (), s32[]{:S(2)}) async-start(), calls=%async_computation.9 | async-start | bytes 1474560 | tf_op jit(solution)/shard_map/all_gather | solution.py:166
  14.1 183.2 %copy-start.160 = (bf16[2048,32]{0,1:T(8,128)(2,1)S(1)}, bf16[2048,32]{0,1:T(8,128)(2,1)}, u32[]{:S(2)}) copy-start(bf16[2048,32]{0,1:T(8,128)(2,1)} %param.57) | copy-start | bytes 393220
  14.1 1244.0 %all-gather.35.cloned.1.call-start = ((), (), s32[]{:S(2)}) async-start(), calls=%async_computation.7 | async-start | bytes 1474560 | tf_op jit(solution)/shard_map/all_gather | solution.py:164
  14.8 207.3 %copy-start.170 = (bf16[32,1536]{1,0:T(8,128)(2,1)S(1)}, bf16[32,1536]{1,0:T(8,128)(2,1)}, u32[]{:S(2)}) copy-start(bf16[32,1536]{1,0:T(8,128)(2,1)} %param.58) | copy-start | bytes 294916
  14.8 230.0 %copy-start.209 = (bf16[384]{0:T(512)(128)(2,1)S(1)}, bf16[384]{0:T(512)(128)(2,1)}, u32[]{:S(2)}) copy-start(bf16[384]{0:T(512)(128)(2,1)} %param.47) | copy-start | bytes 2308
  14.9 242.7 %copy-start.171 = (bf16[1536,32]{0,1:T(8,128)(2,1)S(1)}, bf16[1536,32]{0,1:T(8,128)(2,1)}, u32[]{:S(2)}) copy-start(bf16[1536,32]{0,1:T(8,128)(2,1)} %param.61) | copy-start | bytes 294916
  14.9 263.6 %copy-start.172 = (bf16[1536,32]{0,1:T(8,128)(2,1)S(1)}, bf16[1536,32]{0,1:T(8,128)(2,1)}, u32[]{:S(2)}) copy-start(bf16[1536,32]{0,1:T(8,128)(2,1)} %param.59) | copy-start | bytes 294916
  14.9 285.8 %copy-start.173 = (bf16[32,1536]{1,0:T(8,128)(2,1)S(1)}, bf16[32,1536]{1,0:T(8,128)(2,1)}, u32[]{:S(2)}) copy-start(bf16[32,1536]{1,0:T(8,128)(2,1)} %param.64) | copy-start | bytes 294916
  14.9 1487.7 %all-gather.41.cloned.1.call-start = ((), (), s32[]{:S(2)}) async-start(), calls=%async_computation.10 | async-start | bytes 17694720 | tf_op jit(solution)/shard_map/all_gather | solution.py:232
  15.5 1517.3 %all-gather.43.cloned.1.call-start = ((), (), s32[]{:S(2)}) async-start(), calls=%async_computation.11 | async-start | bytes 1474560 | tf_op jit(solution)/shard_map/all_gather | solution.py:167
  16.2 2531.6 %all-reduce.96.cloned.1.call-start = ((), (), s32[]{:S(2)}) async-start(), calls=%async_computation.15 | async-start | bytes 36175872 | tf_op jit(solution)/shard_map/psum | solution.py:318
  34.7 291.6 %copy-start.177 = (f32[1536]{0:T(1024)}, f32[1536]{0:T(1024)S(1)}, u32[]{:S(2)}) copy-start(f32[1536]{0:T(1024)S(1)} %reshape.246) | copy-start | bytes 18436
  52.7 275.7 %copy-start.72 = (bf16[1536,128]{0,1:T(8,128)(2,1)}, bf16[1536,128]{0,1:T(8,128)(2,1)S(1)}, u32[]{:S(2)}) copy-start(bf16[1536,128]{0,1:T(8,128)(2,1)S(1)} %all_gather.98) | copy-start | bytes 1179652
  76.0 258.5 %copy-start.49 = (bf16[128,2048]{1,0:T(8,128)(2,1)}, bf16[128,2048]{1,0:T(8,128)(2,1)S(1)}, u32[]{:S(2)}) copy-start(bf16[128,2048]{1,0:T(8,128)(2,1)S(1)} %all_gather.99) | copy-start | bytes 1572868
  76.8 321.3 %copy-start.198 = (pred[512]{0:T(512)(128)(4,1)}, pred[512]{0:T(512)(128)(4,1)S(1)}, u32[]{:S(2)}) copy-start(pred[512]{0:T(512)(128)(4,1)S(1)} %get-tuple-element.146) | copy-start | bytes 1540
  93.6 241.7 %copy-start.175 = (f32[1,2048]{1,0:T(1,128)}, f32[1,2048]{1,0:T(1,128)S(1)}, u32[]{:S(2)}) copy-start(f32[1,2048]{1,0:T(1,128)S(1)} %get-tuple-element.140) | copy-start | bytes 24580
  93.6 241.7 %copy-start.179 = (f32[1,2048]{1,0:T(1,128)}, f32[1,2048]{1,0:T(1,128)S(1)}, u32[]{:S(2)}) copy-start(f32[1,2048]{1,0:T(1,128)S(1)} %get-tuple-element.141) | copy-start | bytes 24580
  93.6 241.7 %copy-start.181 = (f32[1,2048]{1,0:T(1,128)}, f32[1,2048]{1,0:T(1,128)S(1)}, u32[]{:S(2)}) copy-start(f32[1,2048]{1,0:T(1,128)S(1)} %get-tuple-element.143) | copy-start | bytes 24580
  93.6 241.7 %copy-start.183 = (f32[1,2048]{1,0:T(1,128)}, f32[1,2048]{1,0:T(1,128)S(1)}, u32[]{:S(2)}) copy-start(f32[1,2048]{1,0:T(1,128)S(1)} %get-tuple-element.142) | copy-start | bytes 24580
  128.3 228.2 %copy-start.46 = (bf16[2048,128]{0,1:T(8,128)(2,1)}, bf16[2048,128]{0,1:T(8,128)(2,1)S(1)}, u32[]{:S(2)}) copy-start(bf16[2048,128]{0,1:T(8,128)(2,1)S(1)} %all_gather.102) | copy-start | bytes 1572868
  156.5 241.7 %copy-start.151 = (f32[2048]{0:T(1024)}, f32[2048]{0:T(1024)S(1)}, u32[]{:S(2)}) copy-start(f32[2048]{0:T(1024)S(1)} %get-tuple-element.145) | copy-start | bytes 24580
  328.4 327.5 %copy-start.12 = (bf16[512,1536]{1,0:T(8,128)(2,1)}, bf16[512,1536]{1,0:T(8,128)(2,1)S(1)}, u32[]{:S(2)}) copy-start(bf16[512,1536]{1,0:T(8,128)(2,1)S(1)} %fusion.33) | copy-start | bytes 4718596
  497.8 41.8 %copy-start.62 = (f32[32,2048]{1,0:T(8,128)}, f32[32,2048]{1,0:T(8,128)S(1)}, u32[]{:S(2)}) copy-start(f32[32,2048]{1,0:T(8,128)S(1)} %slice.342) | copy-start | bytes 786436
  501.5 33.2 %copy-start.76 = (f32[64,2048]{1,0:T(8,128)S(1)}, f32[64,2048]{1,0:T(8,128)}, u32[]{:S(2)}) copy-start(f32[64,2048]{1,0:T(8,128)} %get-tuple-element.95) | copy-start | bytes 1572868
  502.6 47.3 %copy-start.111 = (f32[16,2048]{1,0:T(8,128)}, f32[16,2048]{1,0:T(8,128)S(1)}, u32[]{:S(2)}) copy-start(f32[16,2048]{1,0:T(8,128)S(1)} %slice.349) | copy-start | bytes 393220
  505.2 44.6 %copy-start.88 = (f32[16,2048]{1,0:T(8,128)}, f32[16,2048]{1,0:T(8,128)S(1)}, u32[]{:S(2)}) copy-start(f32[16,2048]{1,0:T(8,128)S(1)} %slice.348) | copy-start | bytes 393220
  506.3 43.6 %copy-start.113 = (f32[16,2048]{1,0:T(8,128)}, f32[16,2048]{1,0:T(8,128)S(1)}, u32[]{:S(2)}) copy-start(f32[16,2048]{1,0:T(8,128)S(1)} %slice.352) | copy-start | bytes 393220
  507.3 24.9 copy-start.130
  508.0 47.4 %copy-start.126 = (f32[8,2048]{1,0:T(8,128)}, f32[8,2048]{1,0:T(8,128)S(1)}, u32[]{:S(2)}) copy-start(f32[8,2048]{1,0:T(8,128)S(1)} %slice.354) | copy-start | bytes 196612
  508.1 24.1 copy-start.132
  521.7 33.7 %copy-start.162 = (f32[1,2048]{1,0:T(1,128)}, f32[1,2048]{1,0:T(1,128)S(1)}, u32[]{:S(2)}) copy-start(f32[1,2048]{1,0:T(1,128)S(1)} %get-tuple-element.138) | copy-start | bytes 24580
  528.2 50.0 %copy-start.128 = (f32[7,2048]{1,0:T(8,128)}, f32[7,2048]{1,0:T(8,128)S(1)}, u32[]{:S(2)}) copy-start(f32[7,2048]{1,0:T(8,128)S(1)} %slice.353) | copy-start | bytes 172036
  530.5 48.5 %copy-start.109 = (f32[15,2048]{1,0:T(8,128)}, f32[15,2048]{1,0:T(8,128)S(1)}, u32[]{:S(2)}) copy-start(f32[15,2048]{1,0:T(8,128)S(1)} %slice.347) | copy-start | bytes 368644
  534.8 45.7 %copy-start.77 = (f32[31,2048]{1,0:T(8,128)}, f32[31,2048]{1,0:T(8,128)S(1)}, u32[]{:S(2)}) copy-start(f32[31,2048]{1,0:T(8,128)S(1)} %slice.341) | copy-start | bytes 761860
  556.3 21.9 copy-start.190
  677.1 519.7 %copy-start.14 = (bf16[512,1536]{1,0:T(8,128)(2,1)}, bf16[512,1536]{1,0:T(8,128)(2,1)S(1)}, u32[]{:S(2)}) copy-start(bf16[512,1536]{1,0:T(8,128)(2,1)S(1)} %multiply_convert_fusion.3) | copy-start | bytes 4718596
  677.7 549.2 %copy-start.92 = (bf16[512,128]{1,0:T(8,128)(2,1)}, bf16[512,128]{1,0:T(8,128)(2,1)S(1)}, u32[]{:S(2)}) copy-start(bf16[512,128]{1,0:T(8,128)(2,1)S(1)} %fusion.49) | copy-start | bytes 393220
  678.3 579.7 %copy-start.94 = (bf16[512,128]{1,0:T(8,128)(2,1)}, bf16[512,128]{1,0:T(8,128)(2,1)S(1)}, u32[]{:S(2)}) copy-start(bf16[512,128]{1,0:T(8,128)(2,1)S(1)} %fusion.48) | copy-start | bytes 393220
  720.0 812.8 %copy-start.155 = (bf16[512,128]{1,0:T(8,128)(2,1)}, bf16[512,128]{1,0:T(8,128)(2,1)S(1)}, u32[]{:S(2)}) copy-start(bf16[512,128]{1,0:T(8,128)(2,1)S(1)} %fusion.50) | copy-start | bytes 393220
  1235.9 266.7 %copy-start.42 = (bf16[512,1536]{1,0:T(8,128)(2,1)S(1)}, bf16[512,1536]{1,0:T(8,128)(2,1)}, u32[]{:S(2)}) copy-start(bf16[512,1536]{1,0:T(8,128)(2,1)} %gather_fusion.2) | copy-start | bytes 4718596
  1550.1 25.8 copy-start.25
  1722.8 22.1 copy-start.60
  1727.5 22.2 slice-start.7
  1975.4 794.9 %all-gather.45.cloned.1.call-start = ((), (), s32[]{:S(2)}) async-start(), calls=%async_computation.12 | async-start | bytes 15728640 | tf_op jit(solution)/shard_map/all_gather | solution.py:306
  1992.8 996.1 %all-gather.49.cloned.1.call-start = ((), (), s32[]{:S(2)}) async-start(), calls=%async_computation.14 | async-start | bytes 15728640 | tf_op jit(solution)/shard_map/all_gather | solution.py:307
  (177 other events, 1174.7 us)
Sparse Core Ops, SparseCore 0:
  9.6 143.8 all-gather.20
  155.0 150.7 all-gather.22
  307.4 26.5 all-gather.24
  335.4 27.4 all-gather.26
  364.3 114.8 all-gather.28
  480.6 113.5 all-gather.30
  595.7 113.5 all-gather.46
  710.9 242.1 all-gather.36
  954.7 242.1 all-gather.32
  1198.2 28.6 all-gather.38
  1228.5 29.5 all-gather.34
  1259.5 243.0 all-gather.40
  1504.1 28.6 all-gather.42
  1975.5 572.2 all-reduce.95
  2550.8 219.4 all-gather.44
  2772.4 216.3 all-gather.48
where the time goes:
time: 3020 us; the launch traced here: 3010 us
  waiting for transfers between devices  1740 us (58%)
  local copies, waits for them, and re-layouts  543 us (18%)
  blocking collectives  294 us (10%)
  matrix products  234 us (8%)
  other arithmetic  177 us (6%)
    psum x1, waiting for transfers between devices, local(): lax.psum((grad_down_branch, grad_up_branch, grad_down_gelu, grad_up_gelu,...  528 us
    pad x70, local copies, waits for them, and re-layouts, recurrence(): unused, state = lax.associative_scan(combine, (carried, driven), axis=0)  244 us
    all_gather x1, waiting for transfers between devices, local(): lax.all_gather(feed_down, 'shard', axis=0, tiled=True)  234 us
    all_gather x1, waiting for transfers between devices, local(): lax.all_gather(feed_up, 'shard', axis=1, tiled=True)  233 us
    all_gather x1, waiting for transfers between devices, local(): lax.all_gather(feed_gate, 'shard', axis=1, tiled=True)  231 us
    all_gather x1, waiting for transfers between devices, local(): lax.all_gather(grad_work, 'shard', axis=0, tiled=True)  210 us
    all_gather x1, waiting for transfers between devices, local(): lax.all_gather(work_out, 'shard', axis=0, tiled=True)  207 us
    slice x69, local copies, waits for them, and re-layouts, recurrence(): unused, state = lax.associative_scan(combine, (carried, driven), axis=0)  178 us
  transfers between devices with their start and end apart: 16, of which 11 were waited for; matrix products, arithmetic and copies ran while one was open for 16% of the time, Pallas kernels for 0%

commit v1 on v0

--- a/solution.py
+++ b/solution.py
@@ -9,6 +9,18 @@
 R = 16
 NORM_EPSILON = 1e-06
 DECAY_SCALE = 8.0
+
+
+def collect(value, axis, dim):
+    ways, here, step = (lax.axis_size(axis), lax.axis_index(axis), value.shape[dim])
+    line, have = (value, 1)
+    while have < ways:
+        line = jnp.concatenate(
+            [line, lax.ppermute(line, axis, [(d, (d - have) % ways) for d in range(ways)])],
+            axis=dim,
+        )
+        have = 2 * have
+    return jnp.roll(line, here * step, axis=dim)
 
 
 def matmul(left, right):
@@ -227,7 +239,7 @@
     resid = rows_in + matmul(mixed_low, weight_merge) + extra_merge
     feed_parts = (
         lax.all_gather(norm_second, "shard", axis=0, tiled=True),
-        lax.all_gather(feed_gate, "shard", axis=1, tiled=True),
+        collect(feed_gate, "shard", 1),
         lax.all_gather(feed_up, "shard", axis=1, tiled=True),
         lax.all_gather(feed_down, "shard", axis=0, tiled=True),
     )

time: 3020 us -> 3130 us (1.036)
  blocking collectives: 294 us -> 446 us
  waiting for transfers between devices: 1740 us -> 1600 us
  local copies, waits for them, and re-layouts: 543 us -> 594 us
    all_gather x1 -> x0, waiting for transfers between devices: 231 us -> none  [local(): lax.all_gather(feed_gate, 'shard', axis=1, tiled=True)]
    all_gather x1, blocking collectives: 15.6 us -> 179 us  [local(): lax.all_gather(norm_first, 'shard', axis=0, tiled=True)]
    all_gather x1, waiting for transfers between devices: 0.02 us -> 138 us  [local(): lax.all_gather(merge_weight, 'shard', axis=0, tiled=True)]
  transfers between devices with their start and end apart: 16 -> 17, of which waited for: 11 -> 10; matrix products, arithmetic and copies ran while one was open for 16% -> 18% of each run, Pallas kernels for 0% -> 0%
where the time goes in v1:
time: 3130 us; the launch traced here: 3120 us
  waiting for transfers between devices  1600 us (51%)
  local copies, waits for them, and re-layouts  594 us (19%)
  blocking collectives  446 us (14%)
  matrix products  247 us (8%)
  other arithmetic  199 us (6%)
    psum x1, waiting for transfers between devices, local(): lax.psum((grad_down_branch, grad_up_branch, grad_down_gelu, grad_up_gelu,...  532 us
    pad x70, local copies, waits for them, and re-layouts, recurrence(): unused, state = lax.associative_scan(combine, (carried, driven), axis=0)  244 us
    all_gather x1, waiting for transfers between devices, local(): lax.all_gather(feed_up, 'shard', axis=1, tiled=True)  235 us
    all_gather x1, waiting for transfers between devices, local(): lax.all_gather(feed_down, 'shard', axis=0, tiled=True)  216 us
    all_gather x1, waiting for transfers between devices, local(): lax.all_gather(work_out, 'shard', axis=0, tiled=True)  210 us
    all_gather x1, waiting for transfers between devices, local(): lax.all_gather(grad_work, 'shard', axis=0, tiled=True)  208 us
    slice x69, local copies, waits for them, and re-layouts, recurrence(): unused, state = lax.associative_scan(combine, (carried, driven), axis=0)  199 us
    all_gather x1, blocking collectives, local(): lax.all_gather(norm_first, 'shard', axis=0, tiled=True)  179 us
  transfers between devices with their start and end apart: 17, of which 10 were waited for; matrix products, arithmetic and copies ran while one was open for 18% of the time, Pallas kernels for 0%

profile of v1, /device:TPU:0, one launch (start us, length us, event | category | flops | bytes accessed | tf_op | source)
XLA Modules:
  0.0 3116.5 jit_solution(6743763452970322956)
XLA Ops:
  23.0 178.9 %all-gather.1 = bf16[4,1,384]{2,1,0:T(2,128)(2,1)S(1)} all-gather(bf16[1,1,384]{2,1,0:T(2,128)(2,1)S(1)} %reshape.237), channel_id=1, replica_groups=mesh['rep'=8,'shard'=4] {'shard'}, dimensions={0}, use_global_device_ids=true | all-gather | bytes 3840 | tf_op jit(solution)/shard_map/all_gather | solution.py:145
  202.9 13.2 all_gather.92
  216.1 12.1 all-gather
  228.8 13.4 all-gather.2
  242.8 15.7 all-gather.3
  258.5 11.9 all-gather.4
  273.1 20.5 all_gather.95
  293.6 22.8 all_gather.103
  316.4 20.1 all_gather.107
  336.5 16.3 all_gather.116
  352.8 19.1 all_gather.112
  371.9 16.0 all_gather.109
  388.0 24.0 all_gather.96
  411.9 16.4 all_gather.99
  428.3 20.6 all_gather.104
  448.9 25.2 all_gather.106
  525.0 9.0 copy.113
  537.0 8.2 add_add_fusion
  545.2 9.1 copy.142
  571.9 11.7 exponential_select_fusion
  583.7 9.8 slice.328
  593.4 9.8 slice.324
  603.2 9.8 slice.326
  613.0 9.8 slice.325
  797.2 10.1 slice.388
  807.3 10.0 slice.323
  821.7 8.6 pad.365
  832.6 8.6 pad.364
  850.1 16.6 pad.366
  866.7 16.6 pad.367
  910.3 137.8 %all-gather.30.cloned.1.call-done = bf16[2048,1536]{1,0:T(8,128)(2,1)} async-done(((bf16[512,1536]{1,0:T(8,128)(2,1)}), bf16[2048,1536]{1,0:T(8,128)(2,1)}) %all-gather.30.cloned.1.call-update) | async-done | bytes 6291472 | tf_op jit(solution)/shard_map/all_gather | solution.py:153
  1060.1 19.7 all-gather.32.cloned.1.call-done
  1108.8 215.6 %all-gather.38.cloned.1.call-done = bf16[4608,1536]{1,0:T(8,128)(2,1)} async-done(((bf16[1152,1536]{1,0:T(8,128)(2,1)}), bf16[4608,1536]{1,0:T(8,128)(2,1)}) %all-gather.38.cloned.1.call-update) | async-done | bytes 14155792 | tf_op jit(solution)/shard_map/all_gather | solution.py:244
  1324.4 13.8 fusion.110
  1338.2 16.3 all-gather.40.cloned.1.call-done
  1354.5 9.9 convolution_add_fusion
  1364.4 234.7 %all-gather.34.cloned.1.call-done = bf16[1536,4608]{1,0:T(8,128)(2,1)} async-done(((bf16[1536,1152]{1,0:T(8,128)(2,1)}), bf16[1536,4608]{1,0:T(8,128)(2,1)}) %all-gather.34.cloned.1.call-update) | async-done | bytes 14155792 | tf_op jit(solution)/shard_map/all_gather | solution.py:243
  1599.1 13.5 fusion.145
  1612.6 16.6 all-gather.36.cloned.1.call-done
  1629.2 9.1 convolution_add_fusion.1
  1638.4 34.7 %multiply_convert_fusion = (bf16[512,4608]{1,0:T(8,128)(2,1)}, bf16[512,4608]{1,0:T(8,128)(2,1)}, bf16[512,4608]{1,0:T(8,128)(2,1)}) fusion(f32[512,4608]{1,0:T(8,128)} %convolution_add_fusion, f32[512,4608]{1,0:T(8,128)} %convolution_add_fusion.1, f32[512,4608]{1,0:T(8,128)} %fusion.144, bf16[512,1536]{1,0:T(8,128)(2,1)S(1)} %copy-done.12, ...), kind=kOutput, calls=%fused_computation.18 | convolution fusion | flops 7311458304 | bytes 58195972 | tf_op jit(solution)/shard_map/dot_general | solution.py:27
  1679.2 12.1 fusion.146
  1691.3 13.1 fusion.39
  1723.4 9.9 slice.390
  1733.3 10.2 slice.389
  1849.6 8.7 pad.449
  1858.3 8.6 pad.425
  1871.7 10.4 multiply_add_fusion.1
  1885.2 16.5 pad.426
  1901.7 16.7 pad.452
  1918.4 9.0 pad.428
  1927.3 16.6 pad.451
  1944.0 16.7 pad.427
  1960.7 9.1 pad.370
  1969.8 18.3 multiply_multiply_fusion.5
  1993.6 9.8 fusion.49
  2008.7 8.7 fusion.21
  2033.1 8.1 add_add_fusion.3
  2099.0 12.0 convolution_add_fusion.10
  2121.6 531.9 %all-reduce.96.cloned.1.call-done = (f32[1536,128]{0,1:T(8,128)}, f32[128,2048]{1,0:T(8,128)}, f32[1536,128]{0,1:T(8,128)}, f32[128,2048]{1,0:T(8,128)}, f32[204...) async-done(((f32[1536,128]{0,1:T(8,128)}, ...) | async-done | bytes 18087952 | tf_op jit(solution)/shard_map/psum | solution.py:330
  2669.0 207.6 %all-gather.46.cloned.1.call-done = f32[2048,1536]{1,0:T(8,128)} async-done(((f32[512,1536]{1,0:T(8,128)}), f32[2048,1536]{1,0:T(8,128)}) %all-gather.46.cloned.1.call-update) | async-done | bytes 12582928 | tf_op jit(solution)/shard_map/all_gather | solution.py:319
  2876.6 8.3 gather_fusion.3
  2884.9 210.2 %all-gather.42.cloned.1.call-done = f32[2048,1536]{1,0:T(8,128)} async-done(((f32[512,1536]{1,0:T(8,128)}), f32[2048,1536]{1,0:T(8,128)}) %all-gather.42.cloned.1.call-update) | async-done | bytes 12582928 | tf_op jit(solution)/shard_map/all_gather | solution.py:318
  3095.1 9.1 gather_fusion.1
  (770 shorter events, 602.5 us)
Async XLA Ops:
  7.2 488.4 %all-gather.20.cloned.1.call-start = ((), (), s32[]{:S(2)}) async-start(), calls=%async_computation | async-start | bytes 7864320 | tf_op jit(solution)/shard_map/all_gather | solution.py:138
  7.9 498.3 %all-gather.22.cloned.1.call-start = ((), (), s32[]{:S(2)}) async-start(), calls=%async_computation.1 | async-start | bytes 7864320 | tf_op jit(solution)/shard_map/all_gather | solution.py:146
  8.7 509.8 %all-gather.24.cloned.1.call-start = ((), (), s32[]{:S(2)}) async-start(), calls=%async_computation.2 | async-start | bytes 1310720 | tf_op jit(solution)/shard_map/all_gather | solution.py:150
  9.4 527.6 %all-gather.26.cloned.1.call-start = ((), (), s32[]{:S(2)}) async-start(), calls=%async_computation.3 | async-start | bytes 1310720 | tf_op jit(solution)/shard_map/all_gather | solution.py:172
  10.0 873.3 %all-gather.44.cloned.1.call-start = ((), (), s32[]{:S(2)}) async-start(), calls=%async_computation.12 | async-start | bytes 7864320 | tf_op jit(solution)/shard_map/all_gather | solution.py:139
  10.6 887.3 %all-gather.28.cloned.1.call-start = ((), (), s32[]{:S(2)}) async-start(), calls=%async_computation.4 | async-start | bytes 7864320 | tf_op jit(solution)/shard_map/all_gather | solution.py:147
  11.1 1036.9 %all-gather.30.cloned.1.call-start = ((), (), s32[]{:S(2)}) async-start(), calls=%async_computation.5 | async-start | bytes 7864320 | tf_op jit(solution)/shard_map/all_gather | solution.py:153
  11.9 190.7 %copy-start.191 = (s32[1,4]{1,0:T(1,128)S(1)}, s32[1,4]{1,0:T(1,128)}, u32[]{:S(2)}) copy-start(s32[1,4]{1,0:T(1,128)} %param.66) | copy-start | bytes 52
  11.9 1067.8 %all-gather.32.cloned.1.call-start = ((), (), s32[]{:S(2)}) async-start(), calls=%async_computation.6 | async-start | bytes 1474560 | tf_op jit(solution)/shard_map/all_gather | solution.py:176
  12.7 190.2 %copy-start.185 = (bf16[4,512]{1,0:T(4,128)(2,1)S(1)}, bf16[4,512]{1,0:T(4,128)(2,1)}, u32[]{:S(2)}) copy-start(bf16[4,512]{1,0:T(4,128)(2,1)} %param.41) | copy-start | bytes 12292
  12.7 203.4 %copy-start.187 = (bf16[512]{0:T(512)(128)(2,1)S(1)}, bf16[512]{0:T(512)(128)(2,1)}, u32[]{:S(2)}) copy-start(bf16[512]{0:T(512)(128)(2,1)} %param.42) | copy-start | bytes 3076
  12.7 216.1 %copy-start.186 = (bf16[4,256]{1,0:T(4,128)(2,1)S(1)}, bf16[4,256]{1,0:T(4,128)(2,1)}, u32[]{:S(2)}) copy-start(bf16[4,256]{1,0:T(4,128)(2,1)} %param.44) | copy-start | bytes 6148
  12.7 230.1 %copy-start.188 = (bf16[512]{0:T(512)(128)(2,1)S(1)}, bf16[512]{0:T(512)(128)(2,1)}, u32[]{:S(2)}) copy-start(bf16[512]{0:T(512)(128)(2,1)} %param.45) | copy-start | bytes 3076
  12.7 245.8 %copy-start.190 = (bf16[384]{0:T(512)(128)(2,1)S(1)}, bf16[384]{0:T(512)(128)(2,1)}, u32[]{:S(2)}) copy-start(bf16[384]{0:T(512)(128)(2,1)} %param.47) | copy-start | bytes 2308
  12.7 260.4 %copy-start.139 = (bf16[1536,32]{0,1:T(8,128)(2,1)S(1)}, bf16[1536,32]{0,1:T(8,128)(2,1)}, u32[]{:S(2)}) copy-start(bf16[1536,32]{0,1:T(8,128)(2,1)} %param.51) | copy-start | bytes 294916
  12.7 280.9 %copy-start.140 = (bf16[1536,32]{0,1:T(8,128)(2,1)S(1)}, bf16[1536,32]{0,1:T(8,128)(2,1)}, u32[]{:S(2)}) copy-start(bf16[1536,32]{0,1:T(8,128)(2,1)} %param.53) | copy-start | bytes 294916
  12.7 303.6 %copy-start.141 = (bf16[32,1536]{1,0:T(8,128)(2,1)S(1)}, bf16[32,1536]{1,0:T(8,128)(2,1)}, u32[]{:S(2)}) copy-start(bf16[32,1536]{1,0:T(8,128)(2,1)} %param.58) | copy-start | bytes 294916
  12.8 1311.7 %all-gather.38.cloned.1.call-start = ((), (), s32[]{:S(2)}) async-start(), calls=%async_computation.9 | async-start | bytes 17694720 | tf_op jit(solution)/shard_map/all_gather | solution.py:244
  13.5 323.0 %copy-start.142 = (bf16[32,1536]{1,0:T(8,128)(2,1)S(1)}, bf16[32,1536]{1,0:T(8,128)(2,1)}, u32[]{:S(2)}) copy-start(bf16[32,1536]{1,0:T(8,128)(2,1)} %param.64) | copy-start | bytes 294916
  13.5 339.3 %copy-start.143 = (bf16[1536,32]{0,1:T(8,128)(2,1)S(1)}, bf16[1536,32]{0,1:T(8,128)(2,1)}, u32[]{:S(2)}) copy-start(bf16[1536,32]{0,1:T(8,128)(2,1)} %param.61) | copy-start | bytes 294916
  13.5 358.4 %copy-start.144 = (bf16[1536,32]{0,1:T(8,128)(2,1)S(1)}, bf16[1536,32]{0,1:T(8,128)(2,1)}, u32[]{:S(2)}) copy-start(bf16[1536,32]{0,1:T(8,128)(2,1)} %param.59) | copy-start | bytes 294916
  13.5 374.5 %copy-start.130 = (bf16[32,2048]{1,0:T(8,128)(2,1)S(1)}, bf16[32,2048]{1,0:T(8,128)(2,1)}, u32[]{:S(2)}) copy-start(bf16[32,2048]{1,0:T(8,128)(2,1)} %param.52) | copy-start | bytes 393220
  13.5 1340.9 %all-gather.40.cloned.1.call-start = ((), (), s32[]{:S(2)}) async-start(), calls=%async_computation.10 | async-start | bytes 1474560 | tf_op jit(solution)/shard_map/all_gather | solution.py:179
  14.1 397.8 %copy-start.131 = (bf16[2048,32]{0,1:T(8,128)(2,1)S(1)}, bf16[2048,32]{0,1:T(8,128)(2,1)}, u32[]{:S(2)}) copy-start(bf16[2048,32]{0,1:T(8,128)(2,1)} %param.55) | copy-start | bytes 393220
  14.1 414.2 %copy-start.132 = (bf16[32,2048]{1,0:T(8,128)(2,1)S(1)}, bf16[32,2048]{1,0:T(8,128)(2,1)}, u32[]{:S(2)}) copy-start(bf16[32,2048]{1,0:T(8,128)(2,1)} %param.54) | copy-start | bytes 393220
  14.1 434.7 %copy-start.133 = (bf16[2048,32]{0,1:T(8,128)(2,1)S(1)}, bf16[2048,32]{0,1:T(8,128)(2,1)}, u32[]{:S(2)}) copy-start(bf16[2048,32]{0,1:T(8,128)(2,1)} %param.57) | copy-start | bytes 393220
  14.2 1585.0 %all-gather.34.cloned.1.call-start = ((), (), s32[]{:S(2)}) async-start(), calls=%async_computation.7 | async-start | bytes 17694720 | tf_op jit(solution)/shard_map/all_gather | solution.py:243
  14.9 1614.3 %all-gather.36.cloned.1.call-start = ((), (), s32[]{:S(2)}) async-start(), calls=%async_computation.8 | async-start | bytes 1474560 | tf_op jit(solution)/shard_map/all_gather | solution.py:178
  14.9 464.6 %collective-permute-start = (bf16[1536,1152]{1,0:T(8,128)(2,1)}, bf16[1536,1152]{1,0:T(8,128)(2,1)}, u32[]{:S(2)}, u32[]{:S(2)}) collective-permute-start(bf16[1536,1152]{1,0:T(8,128)(2,1)} %param.48), channel_id=1, source_target_pairs={{0,3},{1,0},{2,1},{3,2},{4,7},{5,4},{6,5},{7,6},{8,11},{9,8},{10,9... | collective-permute-start | bytes 10616840 | tf_op jit(solution)/shard_map/ppermute | solution.py:19
  20.1 2633.5 %all-reduce.96.cloned.1.call-start = ((), (), s32[]{:S(2)}) async-start(), calls=%async_computation.14 | async-start | bytes 36175872 | tf_op jit(solution)/shard_map/psum | solution.py:330
  22.9 456.6 %copy-start.166 = (f32[512]{0:T(512)}, f32[512]{0:T(512)S(1)}, u32[]{:S(2)}) copy-start(f32[512]{0:T(512)S(1)} %get-tuple-element.147) | copy-start | bytes 6148
  22.9 456.6 %copy-start.168 = (f32[512]{0:T(512)}, f32[512]{0:T(512)S(1)}, u32[]{:S(2)}) copy-start(f32[512]{0:T(512)S(1)} %get-tuple-element.148) | copy-start | bytes 6148
  22.9 456.6 %copy-start.170 = (f32[512]{0:T(512)}, f32[512]{0:T(512)S(1)}, u32[]{:S(2)}) copy-start(f32[512]{0:T(512)S(1)} %get-tuple-element.149) | copy-start | bytes 6148
  201.9 302.0 %copy-start.148 = (f32[1536]{0:T(1024)}, f32[1536]{0:T(1024)S(1)}, u32[]{:S(2)}) copy-start(f32[1536]{0:T(1024)S(1)} %reshape.246) | copy-start | bytes 18436
  273.1 222.5 %copy-start.177 = (s32[1024]{0:T(1024)}, s32[1024]{0:T(1024)S(1)}, u32[]{:S(2)}) copy-start(s32[1024]{0:T(1024)S(1)} %pad_clamp_fusion.1) | copy-start | bytes 12292
  474.1 29.9 copy-start.159
  474.7 97.2 %copy-start.128 = (f32[2048]{0:T(1024)}, f32[2048]{0:T(1024)S(1)}, u32[]{:S(2)}) copy-start(f32[2048]{0:T(1024)S(1)} %get-tuple-element.145) | copy-start | bytes 24580
  475.4 37.4 %copy-start.146 = (f32[1,2048]{1,0:T(1,128)}, f32[1,2048]{1,0:T(1,128)S(1)}, u32[]{:S(2)}) copy-start(f32[1,2048]{1,0:T(1,128)S(1)} %get-tuple-element.140) | copy-start | bytes 24580
  486.0 600.0 %collective-permute-start.1 = (bf16[1536,2304]{1,0:T(8,128)(2,1)}, bf16[1536,2304]{1,0:T(8,128)(2,1)}, u32[]{:S(2)}, u32[]{:S(2)}) collective-permute-start(bf16[1536,2304]{1,0:T(8,128)(2,1)} %pad_maximum_fusion), channel_id=1, source_target_pairs={{0,2},{1,3},{2,0},{3,1},{4,6},{5,7},{6,4},{7,5},{8,10},{9,11},{10,... | collective-permute-start | bytes 21233672 | tf_op jit(solution)/shard_map/ppermute | solution.py:19
  503.3 544.7 %copy-start.14 = (bf16[512,1536]{1,0:T(8,128)(2,1)}, bf16[512,1536]{1,0:T(8,128)(2,1)S(1)}, u32[]{:S(2)}) copy-start(bf16[512,1536]{1,0:T(8,128)(2,1)S(1)} %gather_fusion) | copy-start | bytes 4718596
  505.6 392.3 %copy-start.9 = (bf16[512,1536]{1,0:T(8,128)(2,1)}, bf16[512,1536]{1,0:T(8,128)(2,1)S(1)}, u32[]{:S(2)}) copy-start(bf16[512,1536]{1,0:T(8,128)(2,1)S(1)} %fusion.46) | copy-start | bytes 4718596
  690.3 58.1 %copy-start.83 = (f32[16,2048]{1,0:T(8,128)}, f32[16,2048]{1,0:T(8,128)S(1)}, u32[]{:S(2)}) copy-start(f32[16,2048]{1,0:T(8,128)S(1)} %slice.348) | copy-start | bytes 393220
  718.5 45.7 %copy-start.126 = (f32[2,2048]{1,0:T(2,128)}, f32[2,2048]{1,0:T(2,128)S(1)}, u32[]{:S(2)}) copy-start(f32[2,2048]{1,0:T(2,128)S(1)} %slice.366) | copy-start | bytes 49156
  757.0 25.0 copy-start.78
  866.7 16.6 copy-start.178
  903.6 144.4 %copy-start.160 = (pred[512]{0:T(512)(128)(4,1)S(1)}, pred[512]{0:T(512)(128)(4,1)}, u32[]{:S(2)}) copy-start(pred[512]{0:T(512)(128)(4,1)} %copy-done.159) | copy-start | bytes 1540
  910.3 144.4 %copy-start.100 = (bf16[512,128]{1,0:T(8,128)(2,1)}, bf16[512,128]{1,0:T(8,128)(2,1)S(1)}, u32[]{:S(2)}) copy-start(bf16[512,128]{1,0:T(8,128)(2,1)S(1)} %fusion.56) | copy-start | bytes 393220
  1055.4 652.6 %copy-start.4 = (f32[512,1536]{1,0:T(8,128)}, f32[512,1536]{1,0:T(8,128)S(1)}, u32[]{:S(2)}) copy-start(f32[512,1536]{1,0:T(8,128)S(1)} %get-tuple-element.154) | copy-start | bytes 9437188
  1057.5 571.7 %copy-start.87 = (bf16[512,128]{1,0:T(8,128)(2,1)}, bf16[512,128]{1,0:T(8,128)(2,1)S(1)}, u32[]{:S(2)}) copy-start(bf16[512,128]{1,0:T(8,128)(2,1)S(1)} %fusion.62) | copy-start | bytes 393220
  1638.4 34.7 %copy-start.52 = (bf16[128,4608]{1,0:T(8,128)(2,1)S(1)}, bf16[128,4608]{1,0:T(8,128)(2,1)}, u32[]{:S(2)}) copy-start(bf16[128,4608]{1,0:T(8,128)(2,1)} %all-gather.32.cloned.1.call-done) | copy-start | bytes 3538948
  1723.4 20.1 copy-start.17
  1788.0 14.6 copy-start.37
  1806.3 19.5 copy-start.81
  1809.1 19.4 copy-start.29
  1809.1 19.4 copy-start.31
  1809.1 19.4 slice-start.10
  1844.6 22.3 copy-start.55
  1849.6 22.1 copy-start.19
  1849.6 22.1 slice-start.9
  1901.7 16.7 copy-start.33
  1944.0 16.7 copy-start.32
  2041.9 24.7 slice-start.6
  2081.0 795.7 %all-gather.46.cloned.1.call-start = ((), (), s32[]{:S(2)}) async-start(), calls=%async_computation.13 | async-start | bytes 15728640 | tf_op jit(solution)/shard_map/all_gather | solution.py:319
  2099.0 996.2 %all-gather.42.cloned.1.call-start = ((), (), s32[]{:S(2)}) async-start(), calls=%async_computation.11 | async-start | bytes 15728640 | tf_op jit(solution)/shard_map/all_gather | solution.py:318
  (160 other events, 747.5 us)
Sparse Core Ops, SparseCore 0:
  9.6 187.8 all-gather.19
  199.1 139.9 all-gather.21
  340.6 35.2 all-gather.23
  377.3 37.8 all-gather.25
  416.6 315.6 all-gather.43
  733.7 164.1 all-gather.27
  899.5 148.5 all-gather.29
  1049.6 30.0 all-gather.31
  1081.3 243.0 all-gather.37
  1325.8 28.6 all-gather.39
  1356.1 243.0 all-gather.33
  1600.6 28.6 all-gather.35
  2081.1 572.3 all-reduce.95
  2657.1 219.4 all-gather.45
  2878.7 216.3 all-gather.41
